TPU v7x, 512 devices: a whole 4x4x16 slice. The times are simulated.
512 devices in a mesh: line: 16 (over z), bus: 32 (over x, y, core).
Axes of the slice: x: 4, y: 4, z: 16, core: 2. Of those that a mesh axis runs over, the one named last changes fastest.
Arguments:
- transfer_factors: float32 [4096, 65536], P('line', 'bus'), may hold values from -0.24 to 0.24
- line_flows: float32 [4096], P('line'), may hold values from -6 to 6
- from_bus: int32 [4096], replicated, may hold values from 0 to 65535
- to_bus: int32 [4096], replicated, may hold values from 0 to 65535
- tripped: int32 [2, 64], replicated, may hold values from 0 to 4095, as said below
Outputs:
- new_factors: float32 [4096, 65536], P('line', 'bus')
- new_flows: float32 [4096], P('line')
Inputs may be any that keep to these rules, and one draw needn't show every extreme that they name: No line is tripped twice; in every segment at most 8 tripped lines lie in one aligned block of 256 consecutive lines, and some block holds exactly 8.
All inputs are finite; a program needn't handle non-finite values.
Results may differ from a plain program's by a relative error of at most 0.00018.
Values sent between devices are 32-bit elements; how exact they have to be, the bound alone decides.
A program may use at most 64 MiB of HBM per device.

v0:
```python
import jax
import jax.numpy as jnp
from jax import lax
from jax.sharding import PartitionSpec as P


def chol_solve(factor_lower, right):
    middle = lax.linalg.triangular_solve(factor_lower, right, left_side=True, lower=True)
    return lax.linalg.triangular_solve(
        factor_lower, middle, left_side=True, lower=True, transpose_a=True
    )


def column_select(col_global, from_bus, to_bus, outage_ids):
    from_ids = jnp.take(from_bus, outage_ids)
    to_ids = jnp.take(to_bus, outage_ids)
    return (col_global[:, None] == from_ids[None, :]).astype(jnp.float32) - (
        col_global[:, None] == to_ids[None, :]
    ).astype(jnp.float32)


def per_device(transfer_factors, line_flows, from_bus, to_bus, tripped):
    precise = lax.Precision.HIGHEST
    local_rows, local_cols = transfer_factors.shape
    outages = tripped.shape[1]
    line_index = lax.axis_index("line")
    bus_index = lax.axis_index("bus")
    row_global = line_index * local_rows + jnp.arange(local_rows, dtype=jnp.int32)
    col_global = bus_index * local_cols + jnp.arange(local_cols, dtype=jnp.int32)
    factors = transfer_factors
    flows_now = line_flows
    identity = jnp.eye(outages, dtype=jnp.float32)
    for segment_index in range(tripped.shape[0]):
        outage_ids = tripped[segment_index]
        terminal_select = column_select(col_global, from_bus, to_bus, outage_ids)
        outage_select = (outage_ids[:, None] == row_global[None, :]).astype(jnp.float32)
        terminal_part = jnp.dot(factors, terminal_select, precision=precise)
        terminal = lax.psum(terminal_part, "bus")
        outage_terms = lax.psum(jnp.dot(outage_select, terminal, precision=precise), "line")
        outage_rows, outage_flows = lax.psum(
            (
                jnp.dot(outage_select, factors, precision=precise),
                jnp.dot(outage_select, flows_now, precision=precise),
            ),
            "line",
        )
        capacitance = identity - outage_terms
        factor_lower = jnp.linalg.cholesky(jnp.dot(capacitance, capacitance.T, precision=precise))
        update_weights = chol_solve(
            factor_lower, jnp.dot(capacitance, terminal.T, precision=precise)
        )
        factors = factors + jnp.dot(update_weights.T, outage_rows, precision=precise)
        flows_now = flows_now + jnp.dot(update_weights.T, outage_flows, precision=precise)
        keep_mask = 1.0 - jnp.sum(outage_select, axis=0)
        factors = factors * keep_mask[:, None]
        flows_now = flows_now * keep_mask
    return (factors, flows_now)


def solution(mesh):
    placed = (P("line", "bus"), P("line"), P(), P(), P())
    return jax.shard_map(
        per_device,
        mesh=mesh,
        in_specs=placed,
        out_specs=(P("line", "bus"), P("line")),
        check_vma=False,
    )
```

profile of v0, /device:TPU:2, one launch (start us, length us, event | category | flops | bytes accessed | tf_op | source)
XLA Modules:
  0.0 564.4 jit_solution(1560953369744594784)
XLA Ops:
  7.2 0.0 all-reduce.7.cloned.1.call-start
  7.3 0.8 compare_select_fusion
  8.1 0.8 gather_fusion.1
  8.9 1.5 gather_fusion
  10.4 4.6 convolution_bitcast_fusion
  15.0 0.0 all-reduce.7.cloned.1.call-update
  15.0 0.0 all-reduce.9.cloned.1.call-start
  15.1 1.7 fusion.25
  16.9 0.0 all-reduce.11.cloned.1.call-start
  16.9 0.8 gather_fusion.3
  17.7 0.8 gather_fusion.2
  18.5 0.2 convolution_bitcast_fusion.2
  18.6 0.1 fusion.30
  18.8 126.4 %all-reduce.7.cloned.1.call-done = f32[256,64]{0,1:T(8,128)} async-done(((f32[256,64]{0,1:T(8,128)}), f32[256,64]{0,1:T(8,128)}) %all-reduce.7.cloned.1.call-update) | async-done | bytes 65552 | tf_op jit(solution)/shard_map/psum | solution.py:38
  145.2 1.1 fusion.27
  146.3 57.0 %all-reduce.1 = (f32[64,64]{1,0:T(8,128)S(1)}, f32[64]{0:T(128)S(1)}) all-reduce(f32[64,64]{1,0:T(8,128)S(1)} %fusion.27, f32[64]{0:T(128)S(1)} %convolution_bitcast_fusion.2), channel_id=1, replica_groups=mesh['line'=16,'bus'=32] {'line'}, use_global_device_ids=true, to_apply=%region_1.3 | all-reduce | flops 4160 | bytes 33280 | tf_op jit(solution)/shard_map/psum | solution.py:39
  203.2 0.2 fusion.60
  203.4 0.1 copy.11
  203.5 5.8 %cholesky.44 = f32[64,64]{1,0:T(8,128)S(1)} custom-call(f32[64,64]{1,0:T(8,128)S(1)} %fusion.46), custom_call_target="Cholesky" | custom-call | tf_op jit(solution)/shard_map/jit(cholesky)/cholesky | solution.py:48
  209.4 0.6 compare_reduce_fusion.1
  210.0 0.7 fusion.35
  210.7 4.9 custom-call.11
  215.6 1.1 fusion.59
  216.7 0.3 fusion.42
  216.9 0.2 fusion.44
  217.1 0.1 fusion.33
  217.3 0.2 convolution_bitcast_fusion.1
  217.5 67.4 %all-reduce.9.cloned.1.call-done = f32[64,2048]{1,0:T(8,128)} async-done(((f32[64,2048]{1,0:T(8,128)}), f32[64,2048]{1,0:T(8,128)}) %all-reduce.9.cloned.1.call-update) | async-done | bytes 524304 | tf_op jit(solution)/shard_map/psum | solution.py:40
  284.8 3.7 fusion.1
  288.5 3.0 fusion.2
  291.5 0.0 all-reduce.13.cloned.1.call-start
  291.5 1.7 fusion.20
  293.3 120.7 %all-reduce.11.cloned.1.call-done = f32[256,64]{0,1:T(8,128)} async-done(((f32[256,64]{0,1:T(8,128)}), f32[256,64]{0,1:T(8,128)}) %all-reduce.11.cloned.1.call-update) | async-done | bytes 65552 | tf_op jit(solution)/shard_map/psum | solution.py:38
  414.0 1.1 fusion.22
  415.1 56.9 %all-reduce = (f32[64,64]{1,0:T(8,128)S(1)}, f32[64]{0:T(128)S(1)}) all-reduce(f32[64,64]{1,0:T(8,128)S(1)} %fusion.22, f32[64]{0:T(128)S(1)} %convolution_bitcast_fusion.1), channel_id=1, replica_groups=mesh['line'=16,'bus'=32] {'line'}, use_global_device_ids=true, to_apply=%region_7.12 | all-reduce | flops 4160 | bytes 33280 | tf_op jit(solution)/shard_map/psum | solution.py:39
  472.0 0.2 fusion.62
  472.2 0.1 copy.12
  472.3 5.8 %cholesky.55 = f32[64,64]{1,0:T(8,128)S(1)} custom-call(f32[64,64]{1,0:T(8,128)S(1)} %fusion.41), custom_call_target="Cholesky" | custom-call | tf_op jit(solution)/shard_map/jit(cholesky)/cholesky | solution.py:48
  478.1 0.6 compare_reduce_fusion
  478.8 0.7 fusion.36
  479.5 4.9 custom-call.13
  484.3 1.1 fusion.61
  485.4 0.3 fusion.37
  485.7 0.2 fusion.39
  485.9 0.1 fusion.31
  486.0 0.6 add_multiply_fusion
  486.6 67.0 %all-reduce.13.cloned.1.call-done = f32[64,2048]{1,0:T(8,128)} async-done(((f32[64,2048]{1,0:T(8,128)}), f32[64,2048]{1,0:T(8,128)}) %all-reduce.13.cloned.1.call-update) | async-done | bytes 524304 | tf_op jit(solution)/shard_map/psum | solution.py:40
  553.6 4.3 fusion
  (24 shorter events, 0.2 us)
Async XLA Ops:
  7.2 0.9 copy-start
  7.2 7.9 %copy-start.3 = (s32[2,64]{1,0:T(2,128)S(1)}, s32[2,64]{1,0:T(2,128)}, u32[]{:S(2)}) copy-start(s32[2,64]{1,0:T(2,128)} %param.16) | copy-start | bytes 1540
  7.2 7.9 %copy-start.2 = (f32[256,2048]{1,0:T(8,128)S(1)}, f32[256,2048]{1,0:T(8,128)}, u32[]{:S(2)}) copy-start(f32[256,2048]{1,0:T(8,128)} %param.12) | copy-start | bytes 6291460
  7.2 138.0 %all-reduce.7.cloned.1.call-start = ((), (), s32[]{:S(2)}) async-start(), calls=%async_computation | async-start | bytes 131072 | tf_op jit(solution)/shard_map/psum | solution.py:38
  15.0 2.7 copy-start.1
  15.0 269.8 %all-reduce.9.cloned.1.call-start = ((), (), s32[]{:S(2)}) async-start(), calls=%async_computation.1 | async-start | bytes 1048576 | tf_op jit(solution)/shard_map/psum | solution.py:40
  15.1 3.4 copy-start.4
  16.9 397.1 %all-reduce.11.cloned.1.call-start = ((), (), s32[]{:S(2)}) async-start(), calls=%async_computation.2 | async-start | bytes 131072 | tf_op jit(solution)/shard_map/psum | solution.py:38
  291.5 262.2 %all-reduce.13.cloned.1.call-start = ((), (), s32[]{:S(2)}) async-start(), calls=%async_computation.3 | async-start | bytes 1048576 | tf_op jit(solution)/shard_map/psum | solution.py:40
Sparse Core Ops, SparseCore 0:
  15.1 130.0 all-reduce.6
  148.2 136.5 all-reduce.8
  291.6 122.3 all-reduce.10
  416.8 136.7 all-reduce.12
where the time goes:
time: 565 us; the launch traced here: 564 us
  waiting for transfers between devices  382 us (68%)
  blocking collectives  114 us (20%)
  other arithmetic  25.7 us (5%)
  matrix products  25.1 us (4%)
  between operations  14 us (2%)
    psum x2, waiting for transfers between devices, per_device(): terminal = lax.psum(terminal_part, 'bus')  247 us
    psum x2, waiting for transfers between devices, per_device(): lax.psum((jnp.dot(outage_select, factors, precision=precise), jnp.dot(out...  134 us
    psum x2, blocking collectives, per_device(): lax.psum(jnp.dot(outage_select, terminal, precision=precise), 'line')  114 us
    another operation x6, other arithmetic, per_device(): jnp.linalg.cholesky(jnp.dot(capacitance, capacitance.T, precision=precise))  13 us
  transfers between devices with their start and end apart: 4, of which 4 were waited for; matrix products, arithmetic and copies ran while one was open for 6% of the time, Pallas kernels for 0%

commit v1 on v0

--- a/solution.py
+++ b/solution.py
@@ -35,7 +35,7 @@
         terminal_select = column_select(col_global, from_bus, to_bus, outage_ids)
         outage_select = (outage_ids[:, None] == row_global[None, :]).astype(jnp.float32)
         terminal_part = jnp.dot(factors, terminal_select, precision=precise)
-        terminal = lax.psum(terminal_part, "bus")
+        terminal = jnp.sum(lax.all_gather(terminal_part, "bus"), axis=0)
         outage_terms = lax.psum(jnp.dot(outage_select, terminal, precision=precise), "line")
         outage_rows, outage_flows = lax.psum(
             (

time: 565 us -> 317 us (0.56)
  waiting for transfers between devices: 382 us -> 130 us
    psum x2 -> x0, waiting for transfers between devices: 247 us -> none  [per_device(): terminal = lax.psum(terminal_part, 'bus')]
    psum x2, waiting for transfers between devices: 134 us -> 14.5 us  [per_device(): lax.psum((jnp.dot(outage_select, factors, precision=precise), jnp.dot(out...]
    all_gather x0 -> x2, waiting for transfers between devices: none -> 115 us  [per_device(): terminal = jnp.sum(lax.all_gather(terminal_part, 'bus'), axis=0)]
  transfers between devices with their start and end apart: 4 -> 4, of which waited for: 4 -> 4; matrix products, arithmetic and copies ran while one was open for 6% -> 12% of each run, Pallas kernels for 0% -> 0%
where the time goes in v1:
time: 317 us; the launch traced here: 316 us
  waiting for transfers between devices  130 us (41%)
  blocking collectives  114 us (36%)
  other arithmetic  26.2 us (8%)
  matrix products  21.8 us (7%)
  between operations  15.8 us (5%)
  local copies, waits for them, and re-layouts  8.44 us (3%)
    all_gather x2, waiting for transfers between devices, per_device(): terminal = jnp.sum(lax.all_gather(terminal_part, 'bus'), axis=0)  115 us
    psum x2, blocking collectives, per_device(): lax.psum(jnp.dot(outage_select, terminal, precision=precise), 'line')  114 us
    psum x2, waiting for transfers between devices, per_device(): lax.psum((jnp.dot(outage_select, factors, precision=precise), jnp.dot(out...  14.5 us
    another operation x6, other arithmetic, per_device(): jnp.linalg.cholesky(jnp.dot(capacitance, capacitance.T, precision=precise))  13 us
    another operation x4, other arithmetic, chol_solve(): lax.linalg.triangular_solve(factor_lower, middle, left_side=True, lower=T...  11.1 us
    dot_general x2, matrix products, per_device(): jnp.dot(update_weights.T, outage_rows, precision=precise)  7.94 us
    dot_general x2, matrix products, per_device(): terminal_part = jnp.dot(factors, terminal_select, precision=precise)  7.51 us
  transfers between devices with their start and end apart: 4, of which 4 were waited for; matrix products, arithmetic and copies ran while one was open for 12% of the time, Pallas kernels for 0%

profile of v1, /device:TPU:2, one launch (start us, length us, event | category | flops | bytes accessed | tf_op | source)
XLA Modules:
  0.0 316.3 jit_solution(18395131054375255070)
XLA Ops:
  8.1 0.8 compare_select_fusion
  8.9 0.8 gather_fusion
  9.7 1.5 gather_fusion.1
  11.2 4.6 %convolution_bitcast_fusion = f32[256,64]{0,1:T(8,128)} fusion(f32[256,2048]{1,0:T(8,128)} %param.12, s32[64]{0:T(128)S(1)} %get-tuple-element.23, s32[64]{0:T(128)S(1)} %get-tuple-element.22, s32[2048]{0:T(1024)S(1)} %iota_add_fusion), kind=kOutput, calls=%fused_computation.10 | convolution fusion | flops 403308544 | bytes 2171392 | tf_op jit(solution)/shard_map/dot_general | solution.py:37
  15.9 1.7 fusion.25
  17.7 0.8 gather_fusion.2
  18.5 0.8 gather_fusion.3
  19.3 0.2 convolution_bitcast_fusion.2
  19.5 0.1 fusion.30
  19.6 60.6 %all-gather.5.cloned.1.call-done = f32[8192,64]{0,1:T(8,128)} async-done(((f32[256,64]{0,1:T(8,128)}), f32[8192,64]{0,1:T(8,128)}) %all-gather.5.cloned.1.call-update) | async-done | bytes 2097168 | tf_op jit(solution)/shard_map/all_gather | solution.py:38
  80.2 2.2 copy.15
  82.4 0.2 bitcast_reduce_fusion.1
  82.7 0.2 fusion.27
  82.9 57.1 %all-reduce.1 = (f32[64,64]{1,0:T(8,128)S(1)}, f32[64]{0:T(128)S(1)}) all-reduce(f32[64,64]{1,0:T(8,128)S(1)} %fusion.27, f32[64]{0:T(128)S(1)} %convolution_bitcast_fusion.2), channel_id=1, replica_groups=mesh['line'=16,'bus'=32] {'line'}, use_global_device_ids=true, to_apply=%region_1.3 | all-reduce | flops 4160 | bytes 33280 | tf_op jit(solution)/shard_map/psum | solution.py:39
  140.0 0.2 fusion.60
  140.2 0.2 fusion.59
  140.4 0.1 copy.13
  140.5 5.8 %cholesky.44 = f32[64,64]{1,0:T(8,128)S(1)} custom-call(f32[64,64]{1,0:T(8,128)S(1)} %fusion.46), custom_call_target="Cholesky" | custom-call | tf_op jit(solution)/shard_map/jit(cholesky)/cholesky | solution.py:48
  146.3 0.6 compare_reduce_fusion.1
  147.0 0.7 fusion.35
  147.6 4.9 %custom-call.11 = f32[1,64,64]{1,2,0:T(8,128)S(1)} custom-call(f32[1,64,64]{2,1,0:T(8,128)S(1)} %fusion.35), custom_call_target="InvertDiagBlocksLowerTriangular" | custom-call | tf_op jit(solution)/shard_map/triangular_solve/custom-call.2 | solution.py:9
  152.5 0.3 fusion.42
  152.8 0.2 fusion.44
  153.0 0.1 fusion.33
  153.2 7.4 %all-reduce.5.cloned.1.call-done = f32[64,2048]{1,0:T(8,128)} async-done(((f32[64,2048]{1,0:T(8,128)}), f32[64,2048]{1,0:T(8,128)}) %all-reduce.5.cloned.1.call-update) | async-done | bytes 524304 | tf_op jit(solution)/shard_map/psum | solution.py:40
  160.6 3.7 %fusion.1 = f32[256,2048]{1,0:T(8,128)S(1)} fusion(f32[256,2048]{1,0:T(8,128)} %param.12, f32[64,256]{1,0:T(8,128)S(1)} %fusion.44, f32[64,2048]{1,0:T(8,128)} %all-reduce.5.cloned.1.call-done, f32[256]{0:T(256)S(1)} %get-tuple-element.15), kind=kOutput, calls=%fused_computation.7 | convolution fusion | flops 403701760 | bytes 4785152 | tf_op jit(solution)/shard_map/dot_general | solution.py:52
  164.3 2.9 fusion.2
  167.2 0.2 all-reduce.7.cloned.1.call-start
  167.5 0.2 convolution_bitcast_fusion.1
  167.7 1.8 fusion.20
  169.5 54.5 %all-gather.7.cloned.1.call-done = f32[8192,64]{0,1:T(8,128)} async-done(((f32[256,64]{0,1:T(8,128)}), f32[8192,64]{0,1:T(8,128)}) %all-gather.7.cloned.1.call-update) | async-done | bytes 2097168 | tf_op jit(solution)/shard_map/all_gather | solution.py:38
  224.0 2.2 copy.16
  226.2 0.2 bitcast_reduce_fusion
  226.5 0.2 fusion.22
  226.7 57.0 %all-reduce = (f32[64,64]{1,0:T(8,128)S(1)}, f32[64]{0:T(128)S(1)}) all-reduce(f32[64,64]{1,0:T(8,128)S(1)} %fusion.22, f32[64]{0:T(128)S(1)} %convolution_bitcast_fusion.1), channel_id=1, replica_groups=mesh['line'=16,'bus'=32] {'line'}, use_global_device_ids=true, to_apply=%region_7.12 | all-reduce | flops 4160 | bytes 33280 | tf_op jit(solution)/shard_map/psum | solution.py:39
  283.7 0.2 fusion.62
  283.9 0.2 fusion.61
  284.1 0.1 copy.14
  284.2 5.8 %cholesky.55 = f32[64,64]{1,0:T(8,128)S(1)} custom-call(f32[64,64]{1,0:T(8,128)S(1)} %fusion.41), custom_call_target="Cholesky" | custom-call | tf_op jit(solution)/shard_map/jit(cholesky)/cholesky | solution.py:48
  290.1 0.6 compare_reduce_fusion
  290.7 0.7 fusion.36
  291.4 4.9 %custom-call.13 = f32[1,64,64]{1,2,0:T(8,128)S(1)} custom-call(f32[1,64,64]{2,1,0:T(8,128)S(1)} %fusion.36), custom_call_target="InvertDiagBlocksLowerTriangular" | custom-call | tf_op jit(solution)/shard_map/triangular_solve/custom-call.2 | solution.py:9
  296.3 0.3 fusion.37
  296.6 0.2 fusion.39
  296.8 0.1 fusion.31
  296.9 0.6 add_multiply_fusion
  297.5 7.1 %all-reduce.7.cloned.1.call-done = f32[64,2048]{1,0:T(8,128)} async-done(((f32[64,2048]{1,0:T(8,128)}), f32[64,2048]{1,0:T(8,128)}) %all-reduce.7.cloned.1.call-update) | async-done | bytes 524304 | tf_op jit(solution)/shard_map/psum | solution.py:40
  304.6 4.3 %fusion = f32[256,2048]{1,0:T(8,128)} fusion(f32[256,2048]{1,0:T(8,128)S(1)} %fusion.1, f32[64,256]{1,0:T(8,128)S(1)} %fusion.39, f32[64,2048]{1,0:T(8,128)} %all-reduce.7.cloned.1.call-done, f32[256]{0:T(256)S(1)} %get-tuple-element.13), kind=kOutput, calls=%fused_computation.5 | convolution fusion | flops 403701760 | bytes 4785152 | tf_op jit(solution)/shard_map/dot_general | solution.py:52
  (28 shorter events, 0.3 us)
Async XLA Ops:
  8.0 0.9 copy-start
  8.0 7.9 %copy-start.3 = (s32[2,64]{1,0:T(2,128)S(1)}, s32[2,64]{1,0:T(2,128)}, u32[]{:S(2)}) copy-start(s32[2,64]{1,0:T(2,128)} %param.16) | copy-start | bytes 1540
  8.0 7.9 %copy-start.2 = (f32[256,2048]{1,0:T(8,128)S(1)}, f32[256,2048]{1,0:T(8,128)}, u32[]{:S(2)}) copy-start(f32[256,2048]{1,0:T(8,128)} %param.12) | copy-start | bytes 6291460
  8.0 72.2 %all-gather.5.cloned.1.call-start = ((), (), s32[]{:S(2)}) async-start(), calls=%async_computation.2 | async-start | bytes 2162688 | tf_op jit(solution)/shard_map/all_gather | solution.py:38
  15.8 2.7 copy-start.1
  15.8 144.8 %all-reduce.5.cloned.1.call-start = ((), (), s32[]{:S(2)}) async-start(), calls=%async_computation | async-start | bytes 1048576 | tf_op jit(solution)/shard_map/psum | solution.py:40
  15.9 3.4 %copy-start.4 = (f32[256]{0:T(256)S(1)}, f32[256]{0:T(256)}, u32[]{:S(2)}) copy-start(f32[256]{0:T(256)} %param.13) | copy-start | bytes 3076
  17.7 206.3 %all-gather.7.cloned.1.call-start = ((), (), s32[]{:S(2)}) async-start(), calls=%async_computation.3 | async-start | bytes 2162688 | tf_op jit(solution)/shard_map/all_gather | solution.py:38
  167.2 137.4 %all-reduce.7.cloned.1.call-start = ((), (), s32[]{:S(2)}) async-start(), calls=%async_computation.1 | async-start | bytes 1048576 | tf_op jit(solution)/shard_map/psum | solution.py:40
Sparse Core Ops, SparseCore 0:
  15.9 64.2 all-gather.4
  167.4 56.5 all-gather.6
Sparse Core Ops, SparseCore 1:
  19.2 141.4 all-reduce.4
  170.7 133.8 all-reduce.6
